TPU v7x, 32 devices: a whole 2x2x4 slice. The times are simulated.
32 devices in a mesh: panel: 8 (over y, x, core), rep: 4 (over z).
Axes of the slice: x: 2, y: 2, z: 4, core: 2. Of those that a mesh axis runs over, the one named last changes fastest.
Arguments:
- activations: float32 [98304, 1024], P(('panel', 'rep')), may hold values from 0 to 48
- out_grads: float32 [98304, 256], P(('panel', 'rep')), may hold values from -8 to 8
- factor_a: float32 [1024, 1024], P('panel'), may hold values from -7 to 27
- factor_g: float32 [256, 256], P('panel'), may hold values from -7 to 27
- inverse_a: float32 [1024, 1024], P('panel'), may hold values from -0.1875 to 0.1875
- inverse_g: float32 [256, 256], P('panel'), may hold values from -0.375 to 0.375
Outputs:
- new_factor_a: float32 [1024, 1024], P('panel')
- new_factor_g: float32 [256, 256], P('panel')
- precond_grad: float32 [1024, 256], P('panel')
All inputs are finite; a program needn't handle non-finite values.
Results may differ from a plain program's by a relative error of at most 0.000076.
Values sent between devices are 32-bit elements; how exact they have to be, the bound alone decides.
A program may use at most 128 MiB of HBM per device.

v0:
```python
import jax
import jax.numpy as jnp
from jax import lax
from jax.sharding import PartitionSpec as P

decay_rate = 0.6


def gram_rows(left, right):
    return lax.dot_general(
        left,
        right,
        (((0,), (0,)), ((), ())),
        precision=lax.Precision.HIGHEST,
        preferred_element_type=jnp.float32,
    )


def local(activations, out_grads, factor_a, factor_g, inverse_a, inverse_g):
    total_rows = activations.shape[0] * lax.axis_size("panel") * lax.axis_size("rep")
    cin = activations.shape[1]
    joint_part = lax.psum_scatter(
        jnp.concatenate(
            [gram_rows(activations, activations), gram_rows(activations, out_grads)], axis=1
        ),
        "panel",
        scatter_dimension=0,
        tiled=True,
    )
    small_part = lax.psum_scatter(
        gram_rows(out_grads, out_grads), "panel", scatter_dimension=0, tiled=True
    )
    joint, small = lax.psum((joint_part, small_part), "rep")
    new_factor_a = decay_rate * factor_a + (1.0 - decay_rate) * (joint[:, :cin] / total_rows)
    new_factor_g = decay_rate * factor_g + (1.0 - decay_rate) * small
    grad_rows = joint[:, cin:]
    inverse_full = lax.all_gather(inverse_g, "panel", axis=0, tiled=True)
    right = jnp.dot(
        grad_rows, inverse_full, precision=lax.Precision.HIGHEST, preferred_element_type=jnp.float32
    )
    precond_grad = jnp.dot(
        inverse_a,
        lax.all_gather(right, "panel", axis=0, tiled=True),
        precision=lax.Precision.HIGHEST,
        preferred_element_type=jnp.float32,
    )
    return (new_factor_a, new_factor_g, precond_grad)


def solution(mesh):
    in_specs = (
        P(("panel", "rep"), None),
        P(("panel", "rep"), None),
        P("panel", None),
        P("panel", None),
        P("panel", None),
        P("panel", None),
    )
    out_specs = (P("panel", None), P("panel", None), P("panel", None))
    return jax.shard_map(local, mesh=mesh, in_specs=in_specs, out_specs=out_specs, check_vma=False)
```

profile of v0, /device:TPU:0, one launch (start us, length us, event | category | flops | bytes accessed | tf_op | source)
XLA Modules:
  0.0 241.9 jit_solution(12102579174664853631)
XLA Ops:
  7.2 0.0 reduce-scatter.3.cloned.1.call-start
  7.2 45.6 %fusion.3 = f32[1024,1024]{0,1:T(8,128)S(1)} fusion(f32[3072,1024]{1,0:T(8,128)} %param.6), kind=kOutput, calls=%fused_computation.7 | convolution fusion | flops 38654705664 | bytes 16777216 | tf_op jit(solution)/shard_map/dot_general | solution.py:10
  52.9 11.1 %fusion.4 = f32[1024,256]{0,1:T(8,128)S(1)} fusion(f32[3072,1024]{1,0:T(8,128)S(1)} %copy-done.1, f32[3072,256]{1,0:T(8,128)S(1)} %copy-done), kind=kOutput, calls=%fused_computation.8 | convolution fusion | flops 9663676416 | bytes 16777216 | tf_op jit(solution)/shard_map/dot_general | solution.py:10
  64.0 3.4 %pad_maximum_fusion = f32[1024,1280]{0,1:T(8,128)} fusion(f32[1024,256]{0,1:T(8,128)S(1)} %fusion.4, f32[1024,1024]{0,1:T(8,128)S(1)} %fusion.3), kind=kLoop, calls=%fused_computation | loop fusion | flops 1310720 | bytes 10485760 | tf_op jit(solution)/shard_map/concatenate | solution.py:23
  67.4 0.0 reduce-scatter.3.cloned.1.call-update
  67.4 0.0 all-reduce.2.cloned.1.call-start
  67.4 59.2 %reduce-scatter.3.cloned.1.call-done = f32[128,1280]{0,1:T(8,128)} async-done(((f32[1024,1280]{0,1:T(8,128)}), f32[128,1280]{0,1:T(8,128)}) %reduce-scatter.3.cloned.1.call-update) | async-done | bytes 655376 | tf_op jit(solution)/shard_map/reduce_scatter | solution.py:22
  126.7 0.0 all-reduce.2.cloned.1.call-update
  126.7 0.0 reduce-scatter.5.cloned.1.call-start
  126.7 5.8 %fusion.5 = f32[256,256]{1,0:T(8,128)} fusion(f32[3072,256]{1,0:T(8,128)S(1)} %copy-done), kind=kOutput, calls=%fused_computation.9 | convolution fusion | flops 2415919104 | bytes 3407872 | tf_op jit(solution)/shard_map/dot_general | solution.py:10
  132.6 0.0 all-gather.2.cloned.1.call-start
  132.6 9.3 %all_gather.6 = f32[256,256]{1,0:T(8,128)S(1)} all-gather(f32[32,256]{1,0:T(8,128)S(1)} %copy-done.2), channel_id=1, replica_groups=mesh['panel'=8,'rep'=4] {'panel'}, dimensions={0}, use_global_device_ids=true | all-gather | bytes 294912 | tf_op jit(solution)/shard_map/all_gather | solution.py:37
  141.9 27.5 %all-reduce.2.cloned.1.call-done = f32[128,1280]{0,1:T(8,128)} async-done(((f32[128,1280]{0,1:T(8,128)}), f32[128,1280]{0,1:T(8,128)}) %all-reduce.2.cloned.1.call-update) | async-done | bytes 655376 | tf_op jit(solution)/shard_map/psum | solution.py:33
  169.4 1.9 fusion.1
  171.4 0.0 all-gather.2.cloned.1.call-update
  171.4 2.0 copy.9
  173.5 32.3 %reduce-scatter.5.cloned.1.call-done = f32[32,256]{1,0:T(8,128)} async-done(((f32[256,256]{1,0:T(8,128)}), f32[32,256]{1,0:T(8,128)}) %reduce-scatter.5.cloned.1.call-update) | async-done | bytes 32784 | tf_op jit(solution)/shard_map/reduce_scatter | solution.py:30
  205.7 19.6 %psum.15 = f32[32,256]{1,0:T(8,128)S(1)} all-reduce(f32[32,256]{1,0:T(8,128)} %reduce-scatter.5.cloned.1.call-done), channel_id=1, replica_groups=mesh['panel'=8,'rep'=4] {'rep'}, use_global_device_ids=true, to_apply=%region_3.0 | all-reduce | flops 8192 | bytes 65536 | tf_op jit(solution)/shard_map/psum | solution.py:33
  225.3 0.6 multiply_add_fusion
  226.0 2.1 fusion
  228.0 2.0 copy.10
  230.1 1.3 all-gather.2.cloned.1.call-done
  231.4 3.2 %convolution_bitcast_fusion = f32[128,256]{0,1:T(8,128)S(1)} fusion(f32[1024,256]{1,0:T(8,128)} %all-gather.2.cloned.1.call-done, f32[128,1024]{1,0:T(8,128)} %param.10), kind=kOutput, calls=%fused_computation.1 | convolution fusion | flops 402653184 | bytes 1703936 | tf_op jit(solution)/shard_map/dot_general | solution.py:41
  234.6 0.8 copy.11
  (9 shorter events, 0.0 us)
Async XLA Ops:
  7.2 45.7 %copy-start = (f32[3072,256]{1,0:T(8,128)S(1)}, f32[3072,256]{1,0:T(8,128)}, u32[]{:S(2)}) copy-start(f32[3072,256]{1,0:T(8,128)} %param.7) | copy-start | bytes 9437188
  7.2 119.5 %reduce-scatter.3.cloned.1.call-start = ((), (), s32[]{:S(2)}) async-start(), calls=%async_computation.2 | async-start | bytes 5898240 | tf_op jit(solution)/shard_map/reduce_scatter | solution.py:22
  7.2 45.7 %copy-start.1 = (f32[3072,1024]{1,0:T(8,128)S(1)}, f32[3072,1024]{1,0:T(8,128)}, u32[]{:S(2)}) copy-start(f32[3072,1024]{1,0:T(8,128)} %param.6) | copy-start | bytes 37748740
  67.4 65.3 %copy-start.2 = (f32[32,256]{1,0:T(8,128)S(1)}, f32[32,256]{1,0:T(8,128)}, u32[]{:S(2)}) copy-start(f32[32,256]{1,0:T(8,128)} %param.11) | copy-start | bytes 98308
  67.4 157.9 %copy-start.3 = (f32[32,256]{1,0:T(8,128)S(1)}, f32[32,256]{1,0:T(8,128)}, u32[]{:S(2)}) copy-start(f32[32,256]{1,0:T(8,128)} %param.9) | copy-start | bytes 98308
  67.4 102.1 %all-reduce.2.cloned.1.call-start = ((), (), s32[]{:S(2)}) async-start(), calls=%async_computation.3 | async-start | bytes 1310720 | tf_op jit(solution)/shard_map/psum | solution.py:33
  126.7 79.0 %reduce-scatter.5.cloned.1.call-start = ((), (), s32[]{:S(2)}) async-start(), calls=%async_computation.4 | async-start | bytes 294912 | tf_op jit(solution)/shard_map/reduce_scatter | solution.py:30
  132.6 98.8 %all-gather.2.cloned.1.call-start = ((), (), s32[]{:S(2)}) async-start(), calls=%async_computation.5 | async-start | bytes 1179648 | tf_op jit(solution)/shard_map/all_gather | solution.py:43
Sparse Core Ops, SparseCore 0:
  67.5 59.1 reduce-scatter.2
  129.0 40.3 all-reduce.1
  172.5 33.2 reduce-scatter.4
  208.0 23.3 all-gather.1
where the time goes:
time: 242 us
  waiting for transfers between devices  120 us (50%)
  matrix products  67.7 us (28%)
  blocking collectives  28.9 us (12%)
  between operations  13.9 us (6%)
  other arithmetic  6.07 us (3%)
  local copies, waits for them, and re-layouts  4.86 us (2%)
    dot_general x3, matrix products, gram_rows(): lax.dot_general(left, right, (((0,), (0,)), ((), ())), precision=lax.Prec...  62.6 us
    reduce_scatter x1, waiting for transfers between devices, local(): lax.psum_scatter(jnp.concatenate([gram_rows(activations, activations), gr...  59.2 us
    reduce_scatter x1, waiting for transfers between devices, local(): lax.psum_scatter(gram_rows(out_grads, out_grads), 'panel', scatter_dimens...  32.3 us
    psum x1, waiting for transfers between devices, local(): joint, small = lax.psum((joint_part, small_part), 'rep')  27.5 us
    psum x1, blocking collectives, local(): joint, small = lax.psum((joint_part, small_part), 'rep')  19.6 us
    all_gather x1, blocking collectives, local(): inverse_full = lax.all_gather(inverse_g, 'panel', axis=0, tiled=True)  9.27 us
    unnamed x11, local copies, waits for them, and re-layouts  4.86 us
  transfers between devices with their start and end apart: 4, of which 4 were waited for; matrix products, arithmetic and copies ran while one was open for 6% of the time, Pallas kernels for 0%

commit v1 on v0

v1 whole, which is shorter than its diff:
```python
import functools

import jax
import jax.numpy as jnp
from jax import lax
from jax.experimental import pallas as pl
from jax.experimental.pallas import tpu as pltpu
from jax.sharding import PartitionSpec as P

decay_rate = 0.6
MESH = pl.DeviceIdType.MESH
BF = jnp.bfloat16
F32 = jnp.float32
LOAD_ROWS = 256
LOAD_SLOTS = 4
TILE = 512


def split(x):
    hi = x.astype(BF)
    return hi, (x - hi.astype(F32)).astype(BF)


def mm(a, b):
    return jnp.dot(a, b, preferred_element_type=F32)


def mm3(a_hi, a_lo, b_hi, b_lo):
    return mm(a_hi, b_hi) + (mm(a_hi, b_lo) + mm(a_lo, b_hi))


def step_kernel(
    dims, a_hbm, g_hbm, ia_ref, ig_ref, out_a, out_g, out_p,
    a_buf, g_buf, hi, lo, hi_t, lo_t, ig_full, right, *rest,
):
    n_panel, n_rep, rows, cin, cout, chunk_rows = dims
    chunks = len(chunk_rows)
    sums, landed, z_landed, final = (rest[i * chunks : (i + 1) * chunks] for i in range(4))
    (a_sem, g_sem, ig_send, ig_recv, own_sem, h_send, h_recv, z_send, z_recv, f_send, f_recv, r_send, r_recv) = rest[4 * chunks :]
    own, own_g = cin // n_panel, cout // n_panel
    half = cout // 2
    levels = n_panel.bit_length() - 1
    me = lax.axis_index("panel")
    rep = lax.axis_index("rep")

    blocks = rows // LOAD_ROWS

    def a_load(block, slot):
        return pltpu.make_async_copy(
            a_hbm.at[pl.ds(pl.multiple_of(block * LOAD_ROWS, LOAD_ROWS), LOAD_ROWS)], a_buf.at[slot], a_sem.at[slot]
        )

    def g_load(block, slot):
        return pltpu.make_async_copy(
            g_hbm.at[pl.ds(pl.multiple_of(block * LOAD_ROWS, LOAD_ROWS), LOAD_ROWS)], g_buf.at[slot], g_sem.at[slot]
        )

    for block in range(LOAD_SLOTS):
        a_load(block, block).start()
        g_load(block, block).start()

    barrier = pltpu.get_barrier_semaphore()
    for k in range(1, n_panel):
        pl.semaphore_signal(barrier, inc=1, device_id={"panel": me ^ k}, device_id_type=MESH)
    for k in range(1, n_rep):
        pl.semaphore_signal(barrier, inc=1, device_id={"rep": lax.rem(rep + k, n_rep)}, device_id_type=MESH)

    def prepare(block, carry):
        slot = lax.rem(block, LOAD_SLOTS)
        a_load(block, slot).wait()
        g_load(block, slot).wait()
        at = pl.ds(pl.multiple_of(block * LOAD_ROWS, LOAD_ROWS), LOAD_ROWS)
        for piece in range(cin // cout + 1):
            cols = pl.ds(piece * cout, cout)
            x = a_buf[slot, :, cols] if piece < cin // cout else g_buf[slot]
            h, l = split(x)
            hi[at, cols] = h
            lo[at, cols] = l
            h, l = split(x.T)
            hi_t[cols, at] = h
            lo_t[cols, at] = l

        @pl.when(block + LOAD_SLOTS < blocks)
        def _():
            a_load(block + LOAD_SLOTS, slot).start()
            g_load(block + LOAD_SLOTS, slot).start()

        return carry

    lax.fori_loop(0, blocks, prepare, 0)

    pl.semaphore_wait(barrier, n_panel - 1 + n_rep - 1)

    own_copy = pltpu.make_async_copy(ig_ref, ig_full.at[me], own_sem)
    own_copy.start()

    def ig_copy(k):
        return pltpu.make_async_remote_copy(
            ig_ref, ig_full.at[me], ig_send.at[k], ig_recv.at[k], device_id={"panel": me ^ k}, device_id_type=MESH
        )

    for k in range(1, n_panel):
        ig_copy(k).start()

    orders = ([*range(levels)], [0, *reversed(range(1, levels))])

    def slot_of(h, panel):
        slot = 0
        for level, bit in enumerate(orders[h]):
            slot = slot + (((panel >> bit) & 1) << (levels - 1 - level))
        return slot

    def kept(h, level):
        base = 0
        for l in range(level):
            base = base + (((me >> orders[h][l]) & 1) << (levels - 1 - l))
        return base

    def multiply(c, tile):
        first = tile * TILE
        tall = min(TILE, cin + (cout if c == 0 else 0) - first)
        cols = pl.ds(cin if c == 0 else (c - 1) * cout, cout)
        m = pl.ds(first, tall)
        out = mm3(hi_t[m, :], lo_t[m, :], hi[:, cols], lo[:, cols])
        for h in range(2):
            part = out[:, h * half : (h + 1) * half]
            if first < cin:
                for j in range(tall // own):
                    sums[c][h, slot_of(h, first // own + j), :own] = part[j * own : (j + 1) * own]
            else:
                for j in range(n_panel):
                    sums[c][h, slot_of(h, j), pl.ds(own, own_g)] = part[j * own_g : (j + 1) * own_g]
                    if chunk_rows[0] > own + own_g:
                        pad = chunk_rows[0] - own - own_g
                        sums[c][h, slot_of(h, j), pl.ds(own + own_g, pad)] = jnp.zeros((pad, half), F32)

    def halving(c, h, level):
        size = 1 << (levels - 1 - level)
        bit = orders[h][level]
        away = kept(h, level) + (1 - ((me >> bit) & 1)) * size
        return pltpu.make_async_remote_copy(
            sums[c].at[h, pl.ds(away, size)],
            landed[c].at[h, pl.ds(n_panel - 2 * size, size)],
            h_send.at[c, h, level],
            h_recv.at[c, h, level],
            device_id={"panel": me ^ (1 << bit)},
            device_id_type=MESH,
        )

    def add_half(c, h, level):
        size = 1 << (levels - 1 - level)
        at = pl.ds(kept(h, level + 1), size)
        sums[c][h, at] = sums[c][h, at] + landed[c][h, pl.ds(n_panel - 2 * size, size)]

    def part_rows(c, owner):
        tall = chunk_rows[c] // n_rep
        return pl.ds(pl.multiple_of(owner * tall, tall), tall)

    def z_scatter(c, h, k):
        to = lax.rem(rep + k, n_rep)
        return pltpu.make_async_remote_copy(
            sums[c].at[h, slot_of(h, me), part_rows(c, to)],
            z_landed[c].at[k, h],
            z_send.at[c, h, k],
            z_recv.at[c, h, k],
            device_id={"rep": to},
            device_id_type=MESH,
        )

    def z_gather(c, h, k):
        at = part_rows(c, rep)
        return pltpu.make_async_remote_copy(
            final[c].at[h, at],
            final[c].at[h, at],
            f_send.at[c, h, k],
            f_recv.at[c, h, k],
            device_id={"rep": lax.rem(rep + k, n_rep)},
            device_id_type=MESH,
        )

    def right_copy(level, m):
        bit = levels - 1 - level
        return pltpu.make_async_remote_copy(
            right.at[me ^ m],
            right.at[me ^ m],
            r_send.at[level, m >> (bit + 1)],
            r_recv.at[level, m >> (bit + 1)],
            device_id={"panel": me ^ (1 << bit)},
            device_id_type=MESH,
        )

    def right_level(level):
        bit = levels - 1 - level
        return [right_copy(level, m << (bit + 1)) for m in range(1 << level)]

    def stage(c, s):
        if s > 0 and s <= levels:
            for h in range(2):
                halving(c, h, s - 1).wait()
                add_half(c, h, s - 1)
                if s < levels:
                    halving(c, h, s).start()
                else:
                    for k in range(1, n_rep):
                        z_scatter(c, h, k).start()
        elif s == 0:
            for h in range(2):
                halving(c, h, 0).start()
        elif s == levels + 1:
            for h in range(2):
                at = part_rows(c, rep)
                total = sums[c][h, slot_of(h, me), at]
                for k in range(1, n_rep):
                    z_scatter(c, h, k).wait()
                    total = total + z_landed[c][k, h]
                final[c][h, at] = total
                for k in range(1, n_rep):
                    z_gather(c, h, k).start()
        elif s == levels + 2:
            for h in range(2):
                for k in range(1, n_rep):
                    z_gather(c, h, k).wait()
            if c > 0:
                for h in range(2):
                    out_a[:, pl.ds((c - 1) * cout + h * half, half)] = final[c][h, :own]
            else:
                own_copy.wait()
                for k in range(1, n_panel):
                    ig_copy(k).wait()
                ig_hi, ig_lo = split(ig_full[...].reshape(cout, cout))
                acc = jnp.zeros((own, cout), F32)
                for h in range(2):
                    out_g[:, pl.ds(h * half, half)] = final[0][h, pl.ds(own, own_g)]
                    g_hi, g_lo = split(final[0][h, :own])
                    at = slice(h * half, (h + 1) * half)
                    acc = acc + mm3(g_hi, g_lo, ig_hi[at], ig_lo[at])
                right[me] = acc
                for copy in right_level(0):
                    copy.start()
        else:
            level = s - levels - 3
            for copy in right_level(level):
                copy.wait()
            if level + 1 < levels:
                for copy in right_level(level + 1):
                    copy.start()
            else:
                r_hi, r_lo = split(right[...].reshape(cin, cout))
                i_hi, i_lo = split(ia_ref[...])
                out_p[...] = mm3(i_hi, i_lo, r_hi, r_lo)

    waiting = []
    for c in range(chunks):
        tall = cin + (cout if c == 0 else 0)
        tiles = -(-tall // TILE)
        for tile in range(tiles):
            multiply(c, tile)
            if tile == tiles - 1:
                waiting.append([c, 0])
            for item in waiting:
                if item[1] < levels + 3 + (levels if item[0] == 0 else 0):
                    stage(*item)
                    item[1] += 1
    while any(s < levels + 3 + (levels if c == 0 else 0) for c, s in waiting):
        for item in waiting:
            if item[1] < levels + 3 + (levels if item[0] == 0 else 0):
                stage(*item)
                item[1] += 1


def local(activations, out_grads, factor_a, factor_g, inverse_a, inverse_g):
    n_panel, n_rep = lax.axis_size("panel"), lax.axis_size("rep")
    rows, cin = activations.shape
    cout = out_grads.shape[1]
    total_rows = rows * n_panel * n_rep
    own, own_g = cin // n_panel, cout // n_panel
    unit = 8 * n_rep
    chunks = cin // cout + 1
    chunk_rows = (-(-(own + own_g) // unit) * unit,) + (own,) * (chunks - 1)
    levels = n_panel.bit_length() - 1
    half = cout // 2
    dma = pltpu.SemaphoreType.DMA
    dims = (n_panel, n_rep, rows, cin, cout, chunk_rows)
    vmem = pl.BlockSpec(memory_space=pltpu.VMEM)
    hbm = pl.BlockSpec(memory_space=pl.ANY)
    joint, small, precond_grad = pl.pallas_call(
        functools.partial(step_kernel, dims),
        out_shape=(
            jax.ShapeDtypeStruct((own, cin), F32),
            jax.ShapeDtypeStruct((own_g, cout), F32),
            jax.ShapeDtypeStruct((own, cout), F32),
        ),
        in_specs=[hbm, hbm, vmem, vmem],
        out_specs=(vmem, vmem, vmem),
        scratch_shapes=[
            pltpu.VMEM((LOAD_SLOTS, LOAD_ROWS, cin), F32),
            pltpu.VMEM((LOAD_SLOTS, LOAD_ROWS, cout), F32),
            pltpu.VMEM((rows, cin + cout), BF),
            pltpu.VMEM((rows, cin + cout), BF),
            pltpu.VMEM((cin + cout, rows), BF),
            pltpu.VMEM((cin + cout, rows), BF),
            pltpu.VMEM((n_panel, own_g, cout), F32),
            pltpu.VMEM((n_panel, own, cout), F32),
            *[pltpu.VMEM((2, n_panel, r, half), F32) for r in chunk_rows],
            *[pltpu.VMEM((2, n_panel - 1, r, half), F32) for r in chunk_rows],
            *[pltpu.VMEM((n_rep, 2, r // n_rep, half), F32) for r in chunk_rows],
            *[pltpu.VMEM((2, r, half), F32) for r in chunk_rows],
            dma((LOAD_SLOTS,)),
            dma((LOAD_SLOTS,)),
            dma((n_panel,)),
            dma((n_panel,)),
            dma,
            dma((chunks, 2, levels)),
            dma((chunks, 2, levels)),
            dma((chunks, 2, n_rep)),
            dma((chunks, 2, n_rep)),
            dma((chunks, 2, n_rep)),
            dma((chunks, 2, n_rep)),
            dma((levels, n_panel // 2)),
            dma((levels, n_panel // 2)),
        ],
        compiler_params=pltpu.CompilerParams(
            collective_id=0, has_side_effects=True, vmem_limit_bytes=67043328
        ),
    )(activations, out_grads, inverse_a, inverse_g)
    new_factor_a = decay_rate * factor_a + (1.0 - decay_rate) * (joint / total_rows)
    new_factor_g = decay_rate * factor_g + (1.0 - decay_rate) * small
    return (new_factor_a, new_factor_g, precond_grad)


def solution(mesh):
    in_specs = (
        P(("panel", "rep"), None),
        P(("panel", "rep"), None),
        P("panel", None),
        P("panel", None),
        P("panel", None),
        P("panel", None),
    )
    out_specs = (P("panel", None), P("panel", None), P("panel", None))
    return jax.shard_map(local, mesh=mesh, in_specs=in_specs, out_specs=out_specs, check_vma=False)
```

time: 242 us -> 94.3 us (0.39)
  waiting for transfers between devices: 120 us -> 0 us
  Pallas kernels: 0 us -> 88.3 us
  matrix products: 67.7 us -> 0 us
  blocking collectives: 28.9 us -> 0 us
  between operations: 13.9 us -> 0.64 us
  local copies, waits for them, and re-layouts: 4.86 us -> 1.57 us
  other arithmetic: 6.07 us -> 3.49 us
    reduce_scatter x2 -> x0, waiting for transfers between devices: 91.5 us -> none  [the longest x1 59.2 us: local(): lax.psum_scatter(jnp.concatenate([gram_rows(activations, activations), gr...]
    pallas_call x0 -> x1, Pallas kernels: none -> 88.3 us  [local(): pl.pallas_call(functools.partial(step_kernel, dims), out_shape=(jax.Shape...]
    dot_general x5 -> x0, matrix products: 67.7 us -> none  [the longest x3 62.6 us: gram_rows(): lax.dot_general(left, right, (((0,), (0,)), ((), ())), precision=lax.Prec...]
    psum x1 -> x0, waiting for transfers between devices: 27.5 us -> none  [local(): joint, small = lax.psum((joint_part, small_part), 'rep')]
    psum x1 -> x0, blocking collectives: 19.6 us -> none  [local(): joint, small = lax.psum((joint_part, small_part), 'rep')]
    all_gather x1 -> x0, blocking collectives: 9.27 us -> none  [local(): inverse_full = lax.all_gather(inverse_g, 'panel', axis=0, tiled=True)]
    concatenate x1 -> x0, other arithmetic: 3.36 us -> none  [local(): jnp.concatenate([gram_rows(activations, activations), gram_rows(activatio...]
    unnamed x11 -> x1, local copies, waits for them, and re-layouts: 4.86 us -> 1.57 us
  transfers between devices with their start and end apart: 4 -> 0, of which waited for: 4 -> 0; matrix products, arithmetic and copies ran while one was open for 6% -> 0% of each run, Pallas kernels for 0% -> 0%
where the time goes in v1:
time: 94.3 us; the launch traced here: 94 us
  Pallas kernels  88.3 us (94%)
  other arithmetic  3.49 us (4%)
  local copies, waits for them, and re-layouts  1.57 us (2%)
    pallas_call x1, Pallas kernels, local(): pl.pallas_call(functools.partial(step_kernel, dims), out_shape=(jax.Shape...  88.3 us
    add x1, other arithmetic, local(): decay_rate * factor_a + (1.0 - decay_rate) * (joint / total_rows)  2.09 us

profile of v1, /device:TPU:0, one launch (start us, length us, event | category | flops | bytes accessed | tf_op | source)
XLA Modules:
  0.0 94.0 jit_solution(13281709417305005473)
XLA Ops:
  0.6 88.3 %shard_map.85 = (f32[128,1024]{1,0:T(8,128)}, f32[32,256]{1,0:T(8,128)}, f32[128,256]{1,0:T(8,128)}) custom-call(f32[3072,1024]{1,0:T(8,128)} %a_hbm.1, f32[3072,256]{1,0:T(8,128)} %g_hbm.1, f32[128,1024]{1,0:T(8,128)} %ia_ref.1, f32[32,256]{1,0:T(8,128)} %ig_ref.1), custom_call_target="tpu_custom_call" | custom-call | tf_op jit(solution)/shard_map/pallas_call | solution.py:286
  89.0 2.1 %multiply_add_fusion = f32[128,1024]{1,0:T(8,128)} fusion(f32[128,1024]{1,0:T(8,128)} %get-tuple-element.6, f32[128,1024]{1,0:T(8,128)} %param.8), kind=kLoop, calls=%fused_computation | loop fusion | flops 393216 | bytes 1572864 | tf_op jit(solution)/shard_map/add | solution.py:326
  91.1 1.4 %multiply_add_fusion.1 = f32[32,256]{1,0:T(8,128)} fusion(f32[32,256]{1,0:T(8,128)} %get-tuple-element.7, f32[32,256]{1,0:T(8,128)} %param.9), kind=kLoop, calls=%fused_computation.1 | loop fusion | flops 24576 | bytes 98304 | tf_op jit(solution)/shard_map/add | solution.py:327
  92.5 1.6 %copy.10 = f32[128,256]{1,0:T(8,128)} copy(f32[128,256]{1,0:T(8,128)} %get-tuple-element.14) | data formatting | bytes 262144

commit v2 on v1

--- a/solution.py
+++ b/solution.py
@@ -39,9 +39,18 @@
     (a_sem, g_sem, ig_send, ig_recv, own_sem, h_send, h_recv, z_send, z_recv, f_send, f_recv, r_send, r_recv) = rest[4 * chunks :]
     own, own_g = cin // n_panel, cout // n_panel
     half = cout // 2
-    levels = n_panel.bit_length() - 1
+    levels, z_levels = n_panel.bit_length() - 1, n_rep.bit_length() - 1
+    last = levels + 2 * z_levels
     me = lax.axis_index("panel")
     rep = lax.axis_index("rep")
+
+    orders = ([*range(levels)], [0, *reversed(range(1, levels))])
+
+    def slot_of(h, panel):
+        slot = 0
+        for level, bit in enumerate(orders[h]):
+            slot = slot + (((panel >> bit) & 1) << (levels - 1 - level))
+        return slot
 
     blocks = rows // LOAD_ROWS
 
@@ -62,23 +71,35 @@
     barrier = pltpu.get_barrier_semaphore()
     for k in range(1, n_panel):
         pl.semaphore_signal(barrier, inc=1, device_id={"panel": me ^ k}, device_id_type=MESH)
-    for k in range(1, n_rep):
-        pl.semaphore_signal(barrier, inc=1, device_id={"rep": lax.rem(rep + k, n_rep)}, device_id_type=MESH)
+    for level in range(z_levels):
+        pl.semaphore_signal(barrier, inc=1, device_id={"rep": rep ^ (1 << level)}, device_id_type=MESH)
 
     def prepare(block, carry):
         slot = lax.rem(block, LOAD_SLOTS)
         a_load(block, slot).wait()
         g_load(block, slot).wait()
         at = pl.ds(pl.multiple_of(block * LOAD_ROWS, LOAD_ROWS), LOAD_ROWS)
+        g_hi, g_lo = split(g_buf[slot])
         for piece in range(cin // cout + 1):
             cols = pl.ds(piece * cout, cout)
-            x = a_buf[slot, :, cols] if piece < cin // cout else g_buf[slot]
-            h, l = split(x)
-            hi[at, cols] = h
-            lo[at, cols] = l
-            h, l = split(x.T)
-            hi_t[cols, at] = h
-            lo_t[cols, at] = l
+            if piece < cin // cout:
+                x = a_buf[slot, :, cols]
+                h, l = split(x)
+                hi[at, cols] = h
+                lo[at, cols] = l
+                h, l = split(x.T)
+                hi_t[cols, at] = h
+                lo_t[cols, at] = l
+                tall, offset = own, 0
+            else:
+                h, l = split(g_buf[slot].T)
+                tall, offset = own_g, own
+            out = mm3(h, l, g_hi, g_lo)
+            for j in range(cout // tall):
+                panel = j if offset else piece * (cout // own) + j
+                for side in range(2):
+                    dst = sums[0].at[side, slot_of(side, panel), pl.ds(offset, tall)]
+                    dst[...] = dst[...] + out[j * tall : (j + 1) * tall, side * half : (side + 1) * half]
 
         @pl.when(block + LOAD_SLOTS < blocks)
         def _():
@@ -87,9 +108,10 @@
 
         return carry
 
+    sums[0][...] = jnp.zeros_like(sums[0])
     lax.fori_loop(0, blocks, prepare, 0)
 
-    pl.semaphore_wait(barrier, n_panel - 1 + n_rep - 1)
+    pl.semaphore_wait(barrier, n_panel - 1 + z_levels)
 
     own_copy = pltpu.make_async_copy(ig_ref, ig_full.at[me], own_sem)
     own_copy.start()
@@ -101,14 +123,6 @@
 
     for k in range(1, n_panel):
         ig_copy(k).start()
-
-    orders = ([*range(levels)], [0, *reversed(range(1, levels))])
-
-    def slot_of(h, panel):
-        slot = 0
-        for level, bit in enumerate(orders[h]):
-            slot = slot + (((panel >> bit) & 1) << (levels - 1 - level))
-        return slot
 
     def kept(h, level):
         base = 0
@@ -118,21 +132,11 @@
 
     def multiply(c, tile):
         first = tile * TILE
-        tall = min(TILE, cin + (cout if c == 0 else 0) - first)
-        cols = pl.ds(cin if c == 0 else (c - 1) * cout, cout)
-        m = pl.ds(first, tall)
+        m, cols = pl.ds(first, TILE), pl.ds((c - 1) * cout, cout)
         out = mm3(hi_t[m, :], lo_t[m, :], hi[:, cols], lo[:, cols])
         for h in range(2):
-            part = out[:, h * half : (h + 1) * half]
-            if first < cin:
-                for j in range(tall // own):
-                    sums[c][h, slot_of(h, first // own + j), :own] = part[j * own : (j + 1) * own]
-            else:
-                for j in range(n_panel):
-                    sums[c][h, slot_of(h, j), pl.ds(own, own_g)] = part[j * own_g : (j + 1) * own_g]
-                    if chunk_rows[0] > own + own_g:
-                        pad = chunk_rows[0] - own - own_g
-                        sums[c][h, slot_of(h, j), pl.ds(own + own_g, pad)] = jnp.zeros((pad, half), F32)
+            for j in range(TILE // own):
+                sums[c][h, slot_of(h, first // own + j)] = out[j * own : (j + 1) * own, h * half : (h + 1) * half]
 
     def halving(c, h, level):
         size = 1 << (levels - 1 - level)
@@ -152,29 +156,44 @@
         at = pl.ds(kept(h, level + 1), size)
         sums[c][h, at] = sums[c][h, at] + landed[c][h, pl.ds(n_panel - 2 * size, size)]
 
-    def part_rows(c, owner):
-        tall = chunk_rows[c] // n_rep
-        return pl.ds(pl.multiple_of(owner * tall, tall), tall)
-
-    def z_scatter(c, h, k):
-        to = lax.rem(rep + k, n_rep)
-        return pltpu.make_async_remote_copy(
-            sums[c].at[h, slot_of(h, me), part_rows(c, to)],
-            z_landed[c].at[k, h],
-            z_send.at[c, h, k],
-            z_recv.at[c, h, k],
-            device_id={"rep": to},
+    def z_base(c, level):
+        base = 0
+        for l in range(level):
+            base = base + ((rep >> l) & 1) * (chunk_rows[c] >> (l + 1))
+        return base
+
+    def z_rows(c, base, tall):
+        return pl.ds(pl.multiple_of(base, chunk_rows[c] // n_rep), tall)
+
+    def z_scatter(c, h, level):
+        tall = chunk_rows[c] >> (level + 1)
+        away = z_base(c, level) + (1 - ((rep >> level) & 1)) * tall
+        return pltpu.make_async_remote_copy(
+            sums[c].at[h, slot_of(h, me), z_rows(c, away, tall)],
+            z_landed[c].at[h, pl.ds(chunk_rows[c] - 2 * tall, tall)],
+            z_send.at[c, h, level],
+            z_recv.at[c, h, level],
+            device_id={"rep": rep ^ (1 << level)},
             device_id_type=MESH,
         )
 
-    def z_gather(c, h, k):
-        at = part_rows(c, rep)
+    def z_add(c, h, level):
+        tall = chunk_rows[c] >> (level + 1)
+        at = z_rows(c, z_base(c, level + 1), tall)
+        total = sums[c][h, slot_of(h, me), at] + z_landed[c][h, pl.ds(chunk_rows[c] - 2 * tall, tall)]
+        if level + 1 < z_levels:
+            sums[c][h, slot_of(h, me), at] = total
+        else:
+            final[c][h, at] = total
+
+    def z_gather(c, h, level):
+        at = z_rows(c, z_base(c, level + 1), chunk_rows[c] >> (level + 1))
         return pltpu.make_async_remote_copy(
             final[c].at[h, at],
             final[c].at[h, at],
-            f_send.at[c, h, k],
-            f_recv.at[c, h, k],
-            device_id={"rep": lax.rem(rep + k, n_rep)},
+            f_send.at[c, h, level],
+            f_recv.at[c, h, level],
+            device_id={"rep": rep ^ (1 << level)},
             device_id_type=MESH,
         )
 
@@ -194,32 +213,25 @@
         return [right_copy(level, m << (bit + 1)) for m in range(1 << level)]
 
     def stage(c, s):
-        if s > 0 and s <= levels:
+        if s < last:
             for h in range(2):
-                halving(c, h, s - 1).wait()
-                add_half(c, h, s - 1)
+                if 0 < s <= levels:
+                    halving(c, h, s - 1).wait()
+                    add_half(c, h, s - 1)
+                elif levels < s <= levels + z_levels:
+                    z_scatter(c, h, s - levels - 1).wait()
+                    z_add(c, h, s - levels - 1)
+                elif s > levels + z_levels:
+                    z_gather(c, h, last - s).wait()
                 if s < levels:
                     halving(c, h, s).start()
+                elif s < levels + z_levels:
+                    z_scatter(c, h, s - levels).start()
                 else:
-                    for k in range(1, n_rep):
-                        z_scatter(c, h, k).start()
-        elif s == 0:
+                    z_gather(c, h, last - 1 - s).start()
+        elif s == last:
             for h in range(2):
-                halving(c, h, 0).start()
-        elif s == levels + 1:
-            for h in range(2):
-                at = part_rows(c, rep)
-                total = sums[c][h, slot_of(h, me), at]
-                for k in range(1, n_rep):
-                    z_scatter(c, h, k).wait()
-                    total = total + z_landed[c][k, h]
-                final[c][h, at] = total
-                for k in range(1, n_rep):
-                    z_gather(c, h, k).start()
-        elif s == levels + 2:
-            for h in range(2):
-                for k in range(1, n_rep):
-                    z_gather(c, h, k).wait()
+                z_gather(c, h, 0).wait()
             if c > 0:
                 for h in range(2):
                     out_a[:, pl.ds((c - 1) * cout + h * half, half)] = final[c][h, :own]
@@ -238,7 +250,7 @@
                 for copy in right_level(0):
                     copy.start()
         else:
-            level = s - levels - 3
+            level = s - last - 1
             for copy in right_level(level):
                 copy.wait()
             if level + 1 < levels:
@@ -249,23 +261,34 @@
                 i_hi, i_lo = split(ia_ref[...])
                 out_p[...] = mm3(i_hi, i_lo, r_hi, r_lo)
 
-    waiting = []
-    for c in range(chunks):
-        tall = cin + (cout if c == 0 else 0)
-        tiles = -(-tall // TILE)
-        for tile in range(tiles):
+    def cost(c, s):
+        if s == 0:
+            return "core", 1.6, 1.0
+        if s < levels:
+            return "xy", (2.8, 1.4)[min(s - 1, 1)], 1.6
+        if s < last:
+            return "z", 1.4, 1.9
+        return "xy", (1.4, 2.8, 1.6)[min(s - last, 2)], 1.6
+
+    tiles = [(c, tile) for c in range(1, chunks) for tile in range(cin // TILE)]
+    ends = {c: last + (levels if c == 0 else 0) for c in range(chunks)}
+    ready, free, now = {(0, 0): 0.0}, {}, 0.0
+    while ready or tiles:
+        due = [item for item in ready if ready[item] <= now]
+        if not due and tiles:
+            c, tile = tiles.pop(0)
             multiply(c, tile)
-            if tile == tiles - 1:
-                waiting.append([c, 0])
-            for item in waiting:
-                if item[1] < levels + 3 + (levels if item[0] == 0 else 0):
-                    stage(*item)
-                    item[1] += 1
-    while any(s < levels + 3 + (levels if c == 0 else 0) for c, s in waiting):
-        for item in waiting:
-            if item[1] < levels + 3 + (levels if item[0] == 0 else 0):
-                stage(*item)
-                item[1] += 1
+            now += 1.8
+            if tile == cin // TILE - 1:
+                ready[c, 0] = now
+            continue
+        c, s = min(due) if due else min(ready, key=lambda item: (ready[item], item))
+        now = max(now, ready.pop((c, s))) + 0.2
+        stage(c, s)
+        if s < ends[c]:
+            link, busy, lag = cost(c, s)
+            free[link] = max(free.get(link, 0.0), now) + busy
+            ready[c, s + 1] = free[link] + lag
 
 
 def local(activations, out_grads, factor_a, factor_g, inverse_a, inverse_g):
@@ -295,15 +318,15 @@
         scratch_shapes=[
             pltpu.VMEM((LOAD_SLOTS, LOAD_ROWS, cin), F32),
             pltpu.VMEM((LOAD_SLOTS, LOAD_ROWS, cout), F32),
-            pltpu.VMEM((rows, cin + cout), BF),
-            pltpu.VMEM((rows, cin + cout), BF),
-            pltpu.VMEM((cin + cout, rows), BF),
-            pltpu.VMEM((cin + cout, rows), BF),
+            pltpu.VMEM((rows, cin), BF),
+            pltpu.VMEM((rows, cin), BF),
+            pltpu.VMEM((cin, rows), BF),
+            pltpu.VMEM((cin, rows), BF),
             pltpu.VMEM((n_panel, own_g, cout), F32),
             pltpu.VMEM((n_panel, own, cout), F32),
             *[pltpu.VMEM((2, n_panel, r, half), F32) for r in chunk_rows],
             *[pltpu.VMEM((2, n_panel - 1, r, half), F32) for r in chunk_rows],
-            *[pltpu.VMEM((n_rep, 2, r // n_rep, half), F32) for r in chunk_rows],
+            *[pltpu.VMEM((2, r, half), F32) for r in chunk_rows],
             *[pltpu.VMEM((2, r, half), F32) for r in chunk_rows],
             dma((LOAD_SLOTS,)),
             dma((LOAD_SLOTS,)),

time: 94.3 us -> 86.6 us (0.918)
  Pallas kernels: 88.3 us -> 80.7 us
    pallas_call x1, Pallas kernels: 88.3 us -> 80.7 us  [local(): pl.pallas_call(functools.partial(step_kernel, dims), out_shape=(jax.Shape...]
where the time goes in v2:
time: 86.6 us; the launch traced here: 86.3 us
  Pallas kernels  80.7 us (93%)
  other arithmetic  3.49 us (4%)
  local copies, waits for them, and re-layouts  1.57 us (2%)
    pallas_call x1, Pallas kernels, local(): pl.pallas_call(functools.partial(step_kernel, dims), out_shape=(jax.Shape...  80.7 us
    add x1, other arithmetic, local(): decay_rate * factor_a + (1.0 - decay_rate) * (joint / total_rows)  2.09 us

profile of v2, /device:TPU:0, one launch (start us, length us, event | category | flops | bytes accessed | tf_op | source)
XLA Modules:
  0.0 86.3 jit_solution(7224039885540539633)
XLA Ops:
  0.6 80.7 %shard_map.85 = (f32[128,1024]{1,0:T(8,128)}, f32[32,256]{1,0:T(8,128)}, f32[128,256]{1,0:T(8,128)}) custom-call(f32[3072,1024]{1,0:T(8,128)} %a_hbm.1, f32[3072,256]{1,0:T(8,128)} %g_hbm.1, f32[128,1024]{1,0:T(8,128)} %ia_ref.1, f32[32,256]{1,0:T(8,128)} %ig_ref.1), custom_call_target="tpu_custom_call" | custom-call | tf_op jit(solution)/shard_map/pallas_call | solution.py:309
  81.3 2.1 %multiply_add_fusion = f32[128,1024]{1,0:T(8,128)} fusion(f32[128,1024]{1,0:T(8,128)} %get-tuple-element.6, f32[128,1024]{1,0:T(8,128)} %param.8), kind=kLoop, calls=%fused_computation | loop fusion | flops 393216 | bytes 1572864 | tf_op jit(solution)/shard_map/add | solution.py:349
  83.4 1.4 %multiply_add_fusion.1 = f32[32,256]{1,0:T(8,128)} fusion(f32[32,256]{1,0:T(8,128)} %get-tuple-element.7, f32[32,256]{1,0:T(8,128)} %param.9), kind=kLoop, calls=%fused_computation.1 | loop fusion | flops 24576 | bytes 98304 | tf_op jit(solution)/shard_map/add | solution.py:350
  84.8 1.6 %copy.10 = f32[128,256]{1,0:T(8,128)} copy(f32[128,256]{1,0:T(8,128)} %get-tuple-element.14) | data formatting | bytes 262144

commit v3 on v2

--- a/solution.py
+++ b/solution.py
@@ -14,6 +14,7 @@
 LOAD_ROWS = 256
 LOAD_SLOTS = 4
 TILE = 512
+SLACK = 1.0
 
 
 def split(x):
@@ -288,7 +289,13 @@
         if s < ends[c]:
             link, busy, lag = cost(c, s)
             free[link] = max(free.get(link, 0.0), now) + busy
-            ready[c, s + 1] = free[link] + lag
+            ready[c, s + 1] = now + SLACK * (free[link] + lag - now)
+
+
+def blend_kernel(total_rows, joint, small, precond, factor_a, factor_g, out_a, out_g, out_p):
+    out_a[...] = decay_rate * factor_a[...] + (1.0 - decay_rate) * (joint[...] / total_rows)
+    out_g[...] = decay_rate * factor_g[...] + (1.0 - decay_rate) * small[...]
+    out_p[...] = precond[...]
 
 
 def local(activations, out_grads, factor_a, factor_g, inverse_a, inverse_g):
@@ -346,9 +353,12 @@
             collective_id=0, has_side_effects=True, vmem_limit_bytes=67043328
         ),
     )(activations, out_grads, inverse_a, inverse_g)
-    new_factor_a = decay_rate * factor_a + (1.0 - decay_rate) * (joint / total_rows)
-    new_factor_g = decay_rate * factor_g + (1.0 - decay_rate) * small
-    return (new_factor_a, new_factor_g, precond_grad)
+    return pl.pallas_call(
+        functools.partial(blend_kernel, total_rows),
+        out_shape=tuple(jax.ShapeDtypeStruct(x.shape, F32) for x in (joint, small, precond_grad)),
+        in_specs=[vmem] * 5,
+        out_specs=(vmem,) * 3,
+    )(joint, small, precond_grad, factor_a, factor_g)
 
 
 def solution(mesh):

time: 86.6 us -> 83.6 us (0.965)
  other arithmetic: 3.49 us -> 0 us
  Pallas kernels: 80.7 us -> 82.8 us
  local copies, waits for them, and re-layouts: 1.57 us -> 0 us
    add x2 -> x0, other arithmetic: 3.49 us -> none  [the longest x1 2.09 us: local(): decay_rate * factor_a + (1.0 - decay_rate) * (joint / total_rows)]
    pallas_call x0 -> x1, Pallas kernels: none -> 2.18 us  [local(): pl.pallas_call(functools.partial(blend_kernel, total_rows), out_shape=tup...]
    unnamed x1 -> x0, local copies, waits for them, and re-layouts: 1.57 us -> none
where the time goes in v3:
time: 83.6 us; the launch traced here: 83.5 us
  Pallas kernels  82.8 us (99%)
    pallas_call x1, Pallas kernels, local(): pl.pallas_call(functools.partial(step_kernel, dims), out_shape=(jax.Shape...  80.7 us
    pallas_call x1, Pallas kernels, local(): pl.pallas_call(functools.partial(blend_kernel, total_rows), out_shape=tup...  2.18 us

profile of v3, /device:TPU:0, one launch (start us, length us, event | category | flops | bytes accessed | tf_op | source)
XLA Modules:
  0.0 83.5 jit_solution(18292781179923821516)
XLA Ops:
  0.6 80.7 %shard_map.85 = (f32[128,1024]{1,0:T(8,128)}, f32[32,256]{1,0:T(8,128)}, f32[128,256]{1,0:T(8,128)}) custom-call(f32[3072,1024]{1,0:T(8,128)} %a_hbm.1, f32[3072,256]{1,0:T(8,128)} %g_hbm.1, f32[128,1024]{1,0:T(8,128)} %ia_ref.1, f32[32,256]{1,0:T(8,128)} %ig_ref.1), custom_call_target="tpu_custom_call" | custom-call | tf_op jit(solution)/shard_map/pallas_call | solution.py:316
  81.3 2.2 %shard_map.86 = (f32[128,1024]{1,0:T(8,128)}, f32[32,256]{1,0:T(8,128)}, f32[128,256]{1,0:T(8,128)}) custom-call(f32[128,1024]{1,0:T(8,128)} %get-tuple-element.6.joint, f32[32,256]{1,0:T(8,128)} %get-tuple-element.7.small, f32[128,256]{1,0:T(8,128)} %get-tuple-element.8.precond, f32[128,1024]{1,0:T(8,128)} %factor_a.1, f32[32,256]{1,0:T(8,128)} %factor_g.1), custom_call_target="tpu_custom_call" | custom-call | tf_op jit(solution)/shard_map/pallas_call | solution.py:356
